TPU v7x, 32 devices: a whole 2x2x4 slice. The times are simulated.
32 devices in a mesh: gx: 8 (over y, x, core), gy: 4 (over z).
Axes of the slice: x: 2, y: 2, z: 4, core: 2. Of those that a mesh axis runs over, the one named last changes fastest.
Arguments:
- thinker_normed: bfloat16 [4, 16, 8192], P(None, None, 'gx'), may hold values from -6 to 6
- thinker_resid: bfloat16 [4, 16, 8192], P('gy', None, 'gx'), may hold values from -6 to 6
- gate_weight: bfloat16 [8192, 29568], P('gx', 'gy'), may hold values from -0.0625 to 0.0625
- up_weight: bfloat16 [8192, 29568], P('gx', 'gy'), may hold values from -0.0625 to 0.0625
- down_weight: bfloat16 [29568, 8192], P('gy', 'gx'), may hold values from -0.03125 to 0.03125
- bridge_weight: bfloat16 [8192, 3584], P('gx'), may hold values from -0.0625 to 0.0625
- talker_stream: bfloat16 [4, 1536, 3584], P('gy', 'gx'), may hold values from -6 to 6
- norm_gain: float32 [3584], replicated, may hold values from 0.5 to 2
- w_query: bfloat16 [3584, 1792], P(None, 'gy'), may hold values from -0.09375 to 0.09375
- w_key: bfloat16 [3584, 256], P(None, 'gy'), may hold values from -0.09375 to 0.09375
- w_value: bfloat16 [3584, 256], P(None, 'gy'), may hold values from -0.09375 to 0.09375
- a_query: bfloat16 [3584, 64], replicated, may hold values from -0.09375 to 0.09375
- b_query: bfloat16 [64, 1792], replicated, may hold values from -0.75 to 0.75
- a_value: bfloat16 [3584, 64], replicated, may hold values from -0.09375 to 0.09375
- b_value: bfloat16 [64, 256], replicated, may hold values from -0.75 to 0.75
- text_index: int32 [4, 1536], P('gy', 'gx'), may hold values from 0 to 15
- span_offset: int32 [4], P('gy'), may hold values from 1 to 1535
- out_grad: bfloat16 [4, 1536, 1792], P('gy', 'gx'), may hold values from -6 to 6
Outputs:
- attn_out: bfloat16 [4, 1536, 1792], P('gy', 'gx')
- grad_aq: float32 [3584, 64], replicated
- grad_bq: float32 [64, 1792], replicated
- grad_av: float32 [3584, 64], replicated
- grad_bv: float32 [64, 256], replicated
All inputs are finite; a program needn't handle non-finite values.
Results may differ from a plain program's by a relative error of at most 0.035.
Values may be sent and summed in bfloat16 or wider, within the bound.
No kernel may reach another device: no remote copies, remote signals or barrier semaphores. Data moves between devices by JAX's collectives and lax.ppermute only.
A program may use at most 192 MiB of HBM per device.

v0:
```python
import math
import jax
import jax.numpy as jnp
from jax import lax
from jax.sharding import PartitionSpec as P

HEADS = 14
KVH = 2
HD = 128
rope_base = 1000000.0
norm_eps = 1e-06


def angle_tables(first_pos, length):
    position = (first_pos + jnp.arange(length, dtype=jnp.int32)).astype(jnp.float32)
    frequency = rope_base ** (-(2.0 * jnp.arange(HD // 2, dtype=jnp.float32)) / HD)
    angles = position[:, None] * frequency[None, :]
    return (jnp.cos(angles), jnp.sin(angles))


def rotate(tensor, cosine, sine_table, signed):
    layout = (cosine.shape[0],) + (1,) * (tensor.ndim - 2) + (cosine.shape[1],)
    cosine = cosine.reshape(layout)
    sine_part = sine_table.reshape(layout) * signed
    half_width = tensor.shape[-1] // 2
    first_half = tensor[..., :half_width]
    second_half = tensor[..., half_width:]
    return jnp.concatenate(
        [
            first_half * cosine - second_half * sine_part,
            second_half * cosine + first_half * sine_part,
        ],
        axis=-1,
    )


def on_device(
    thinker_normed,
    thinker_resid,
    gate_weight,
    up_weight,
    down_weight,
    bridge_weight,
    talker_stream,
    norm_gain,
    w_query,
    w_key,
    w_value,
    a_query,
    b_query,
    a_value,
    b_value,
    text_index,
    span_offset,
    out_grad,
):
    seq_count, rows_seq, columns = thinker_normed.shape
    normed = thinker_normed.reshape(seq_count * rows_seq, columns)
    ff_local = gate_weight.shape[1]
    block = normed
    gate_part = jnp.dot(block, gate_weight, preferred_element_type=jnp.float32)
    up_part = jnp.dot(block, up_weight, preferred_element_type=jnp.float32)
    both_parts = lax.psum_scatter(
        jnp.concatenate([gate_part, up_part], axis=1), "gx", scatter_dimension=0, tiled=True
    )
    hidden = (jax.nn.silu(both_parts[:, :ff_local]) * both_parts[:, ff_local:]).astype(jnp.bfloat16)
    partial_out = jnp.dot(
        lax.all_gather(hidden, "gx", axis=0, tiled=True),
        down_weight,
        preferred_element_type=jnp.float32,
    )
    summed = lax.psum_scatter(partial_out, "gy", scatter_dimension=0, tiled=True)
    thinker_out = (summed + thinker_resid[0].astype(jnp.float32)).astype(jnp.bfloat16)
    bridge_part = jnp.dot(thinker_out, bridge_weight, preferred_element_type=jnp.float32)
    bridge = lax.psum(bridge_part, "gx").astype(jnp.bfloat16)
    tokens = talker_stream.shape[1]
    groups = HEADS // KVH
    scale = 1.0 / math.sqrt(HD)
    picks = (text_index[0][:, None] == jnp.arange(rows_seq, dtype=jnp.int32)[None, :]).astype(
        jnp.bfloat16
    )
    mixed = talker_stream[0].astype(jnp.float32) + jnp.dot(
        picks, bridge, preferred_element_type=jnp.float32
    )
    normal = (
        mixed * lax.rsqrt(jnp.mean(mixed * mixed, axis=1, keepdims=True) + norm_eps) * norm_gain
    ).astype(jnp.bfloat16)
    low_query = jnp.dot(normal, a_query, preferred_element_type=jnp.float32).astype(jnp.bfloat16)
    low_value = jnp.dot(normal, a_value, preferred_element_type=jnp.float32).astype(jnp.bfloat16)
    slab_rows = lax.all_gather(normal, "gy", axis=0, tiled=True)
    projected = jnp.concatenate(
        [
            jnp.dot(slab_rows, w_query, preferred_element_type=jnp.float32),
            jnp.dot(slab_rows, w_key, preferred_element_type=jnp.float32),
            jnp.dot(slab_rows, w_value, preferred_element_type=jnp.float32),
        ],
        axis=1,
    )
    returned = lax.all_to_all(projected, "gy", split_axis=0, concat_axis=1, tiled=True)
    parcels = returned.reshape(tokens, lax.axis_size("gy"), -1)
    query_cols = w_query.shape[1]
    key_cols = w_key.shape[1]
    base_query = parcels[:, :, :query_cols].reshape(tokens, -1)
    base_key = parcels[:, :, query_cols : query_cols + key_cols].reshape(tokens, -1)
    base_value = parcels[:, :, query_cols + key_cols :].reshape(tokens, -1)
    first_pos = lax.axis_index("gx") * tokens
    cosine, sine_table = angle_tables(first_pos, tokens)
    query_pre = base_query + jnp.dot(low_query, b_query, preferred_element_type=jnp.float32)
    query = rotate(query_pre.reshape(tokens, KVH, groups, HD), cosine, sine_table, 1.0).astype(
        jnp.bfloat16
    )
    key_local = (
        rotate(base_key.reshape(tokens, KVH, HD), cosine, sine_table, 1.0)
        .astype(jnp.bfloat16)
        .reshape(tokens, KVH * HD)
    )
    value_local = (
        base_value + jnp.dot(low_value, b_value, preferred_element_type=jnp.float32)
    ).astype(jnp.bfloat16)
    key_all, value_all = (
        lax.all_gather(key_local, "gx", axis=0, tiled=True),
        lax.all_gather(value_local, "gx", axis=0, tiled=True),
    )
    length = key_all.shape[0]
    key_rows = key_all.reshape(length, KVH, HD)
    value_rows = value_all.reshape(length, KVH, HD)
    query_places = first_pos + jnp.arange(tokens, dtype=jnp.int32)
    key_places = jnp.arange(length, dtype=jnp.int32)
    causal = (key_places[None, :] <= query_places[:, None]) | (key_places[None, :] < span_offset[0])
    scores = (
        jnp.einsum("tkgd,skd->kgts", query, key_rows, preferred_element_type=jnp.float32) * scale
    )
    scores = jnp.where(causal, scores, -1e30)
    row_max = jnp.max(scores, axis=-1, keepdims=True)
    weights = jnp.exp(scores - row_max)
    probs = (weights / jnp.sum(weights, axis=-1, keepdims=True)).astype(jnp.bfloat16)
    attended = jnp.einsum(
        "kgts,skd->tkgd", probs, value_rows, preferred_element_type=jnp.float32
    ).astype(jnp.bfloat16)
    grad_four = out_grad[0].reshape(tokens, KVH, groups, HD)
    inner_prod = jnp.sum(grad_four.astype(jnp.float32) * attended.astype(jnp.float32), axis=-1)
    dprob = jnp.einsum("tkgd,skd->kgts", grad_four, value_rows, preferred_element_type=jnp.float32)
    dscore = (
        probs.astype(jnp.float32) * (dprob - jnp.transpose(inner_prod, (1, 2, 0))[..., None])
    ).astype(jnp.bfloat16)
    dquery = (
        jnp.einsum("kgts,skd->tkgd", dscore, key_rows, preferred_element_type=jnp.float32) * scale
    )
    query_grad = (
        rotate(dquery, cosine, sine_table, -1.0).reshape(tokens, HEADS * HD).astype(jnp.bfloat16)
    )
    block = probs
    term = jnp.einsum("kgts,tkgd->skd", block, grad_four, preferred_element_type=jnp.float32)
    value_grad = lax.psum_scatter(
        term.reshape(lax.axis_size("gx") * tokens, KVH * HD), "gx", scatter_dimension=0, tiled=True
    ).astype(jnp.bfloat16)
    part_bq = jnp.einsum("tr,tc->rc", low_query, query_grad, preferred_element_type=jnp.float32)
    part_bv = jnp.einsum("tr,tc->rc", low_value, value_grad, preferred_element_type=jnp.float32)
    dlow_query = jnp.einsum(
        "tc,rc->tr", query_grad, b_query, preferred_element_type=jnp.float32
    ).astype(jnp.bfloat16)
    dlow_value = jnp.einsum(
        "tc,rc->tr", value_grad, b_value, preferred_element_type=jnp.float32
    ).astype(jnp.bfloat16)
    part_aq = jnp.einsum("td,tr->dr", normal, dlow_query, preferred_element_type=jnp.float32)
    part_av = jnp.einsum("td,tr->dr", normal, dlow_value, preferred_element_type=jnp.float32)
    grad_aq, grad_bq, grad_av, grad_bv = lax.psum(
        (part_aq, part_bq, part_av, part_bv), ("gx", "gy")
    )
    attn_out = attended.reshape(1, tokens, HEADS * HD)
    return (attn_out, grad_aq, grad_bq, grad_av, grad_bv)


def solution(mesh):
    return jax.shard_map(
        on_device,
        mesh=mesh,
        in_specs=(
            P(None, None, "gx"),
            P("gy", None, "gx"),
            P("gx", "gy"),
            P("gx", "gy"),
            P("gy", "gx"),
            P("gx", None),
            P("gy", "gx", None),
            P(),
            P(None, "gy"),
            P(None, "gy"),
            P(None, "gy"),
            P(),
            P(),
            P(),
            P(),
            P("gy", "gx"),
            P("gy"),
            P("gy", "gx", None),
        ),
        out_specs=(P("gy", "gx", None), P(), P(), P(), P()),
        check_vma=False,
    )
```

profile of v0, /device:TPU:0, one launch (start us, length us, event | category | flops | bytes accessed | tf_op | source)
XLA Modules:
  0.0 564.3 jit_solution(9775176805287978987)
XLA Ops:
  7.2 10.2 %fusion.54 = f32[64,7392]{1,0:T(8,128)S(1)} fusion(bf16[64,1024]{1,0:T(8,128)(2,1)} %bitcast.100, bf16[1024,7392]{0,1:T(8,128)(2,1)} %param.20), kind=kOutput, calls=%fused_computation.78 | convolution fusion | flops 968884224 | bytes 17162240 | tf_op jit(solution)/shard_map/dot_general | solution.py:61
  17.4 10.0 %fusion.55 = f32[64,7392]{1,0:T(8,128)S(1)} fusion(bf16[64,1024]{1,0:T(8,128)(2,1)S(1)} %bitcast.101, bf16[1024,7392]{0,1:T(8,128)(2,1)} %param.21), kind=kOutput, calls=%fused_computation.79 | convolution fusion | flops 968884224 | bytes 17162240 | tf_op jit(solution)/shard_map/dot_general | solution.py:62
  27.4 2.5 pad_maximum_fusion
  29.9 52.0 %reduce-scatter.6.cloned.1.call-done = f32[8,14784]{1,0:T(8,128)} async-done(((f32[64,14784]{1,0:T(8,128)}), f32[8,14784]{1,0:T(8,128)}) %reduce-scatter.6.cloned.1.call-update) | async-done | bytes 473104 | tf_op jit(solution)/shard_map/reduce_scatter | solution.py:63
  83.1 10.8 %all_gather.12 = bf16[64,7392]{1,0:T(8,128)(2,1)S(1)} all-gather(bf16[8,7392]{1,0:T(8,128)(2,1)S(1)} %fusion.32), channel_id=1, replica_groups=mesh['gx'=8,'gy'=4] {'gx'}, dimensions={0}, use_global_device_ids=true | all-gather | bytes 1064448 | tf_op jit(solution)/shard_map/all_gather | solution.py:68
  93.9 8.8 %fusion.56 = f32[64,1024]{1,0:T(8,128)} fusion(bf16[64,7392]{1,0:T(8,128)(2,1)S(1)} %all_gather.12, bf16[7392,1024]{1,0:T(8,128)(2,1)} %param.22), kind=kOutput, calls=%fused_computation.80 | convolution fusion | flops 968884224 | bytes 16347136 | tf_op jit(solution)/shard_map/dot_general | solution.py:67
  102.7 20.1 %reduce-scatter.8.cloned.1.call-done = f32[16,1024]{1,0:T(8,128)} async-done(((f32[64,1024]{1,0:T(8,128)}), f32[16,1024]{1,0:T(8,128)}) %reduce-scatter.8.cloned.1.call-update) | async-done | bytes 65552 | tf_op jit(solution)/shard_map/reduce_scatter | solution.py:72
  122.8 4.2 fusion.41
  127.0 25.4 %all-reduce.5 = bf16[16,3584]{1,0:T(8,128)(2,1)S(1)} all-reduce(f32[16,3584]{1,0:T(8,128)S(1)} %fusion.41), channel_id=1, replica_groups=mesh['gx'=8,'gy'=4] {'gx'}, use_global_device_ids=true, to_apply=%region_2.3 | all-reduce | flops 57344 | bytes 344064 | tf_op jit(solution)/shard_map/psum | solution.py:75
  155.9 99.9 %all-gather.2.cloned.1.call-done = bf16[768,3584]{1,0:T(8,128)(2,1)} async-done(((bf16[192,3584]{1,0:T(8,128)(2,1)}), bf16[768,3584]{1,0:T(8,128)(2,1)}) %all-gather.2.cloned.1.call-update) | async-done | bytes 5505040 | tf_op jit(solution)/shard_map/all_gather | solution.py:90
  255.8 5.4 fusion.57
  266.7 4.6 all-to-all-start
  278.7 38.4 %all-to-all-done = f32[4,192,576]{2,1,0:T(8,128)} async-done(((f32[4,192,576]{2,1,0:T(8,128)}), f32[4,192,576]{2,1,0:T(8,128)}, u32[]{:S(2)}, u32[]{:S(2)}) %all-to-all-start) | async-done | bytes 1769504 | tf_op jit(solution)/shard_map/all_to_all | solution.py:99
  322.8 2.5 reshape.208
  332.9 11.6 %all_gather.15 = bf16[1536,256]{1,0:T(8,128)(2,1)} all-gather(bf16[192,256]{1,0:T(8,128)(2,1)S(1)} %copy.50), channel_id=1, replica_groups=mesh['gx'=8,'gy'=4] {'gx'}, dimensions={0}, use_global_device_ids=true | all-gather | bytes 884736 | tf_op jit(solution)/shard_map/all_gather | solution.py:121
  346.8 3.4 subtract_convert_fusion.1
  350.2 10.5 %fusion.53 = (f32[2,7,192]{2,1,0:T(8,128)S(1)}, f32[2,7,192,1536]{3,2,1,0:T(8,128)}) fusion(pred[192,1536]{1,0:T(8,128)(4,1)S(1)} %copy-done.19, bf16[1536,2,128,1]{0,2,3,1:T(8,128)(2,1)} %bitcast.104, bf16[192,2,7,64]{3,0,2,1:T(8,128)(2,1)} %get-tuple-element.10, bf16[192,2,7,64]{3,0,2,1:T(8,128)(2,1)} %get-tuple-element.9), kind=kOutput, calls=%fused_computation.77 | convolution fusion | flops 1074857472 | bytes 18295296 | tf_op jit(solution)/shard_map/sub | solution.py:135
  360.8 7.1 %divide_convert_fusion = bf16[2,7,192,1536]{3,2,1,0:T(8,128)(2,1)S(1)} fusion(f32[2,7,192,1536]{3,2,1,0:T(8,128)} %get-tuple-element.25, f32[2,7,192]{2,1,0:T(8,128)S(1)} %get-tuple-element.24), kind=kLoop, calls=%fused_computation.5 | loop fusion | flops 8257536 | bytes 24783360 | tf_op jit(solution)/shard_map/convert_element_type | solution.py:136
  374.4 11.2 %all_gather.14 = bf16[1536,256]{1,0:T(8,128)(2,1)} all-gather(bf16[192,256]{1,0:T(8,128)(2,1)S(1)} %fusion.22), channel_id=1, replica_groups=mesh['gx'=8,'gy'=4] {'gx'}, dimensions={0}, use_global_device_ids=true | all-gather | bytes 884736 | tf_op jit(solution)/shard_map/all_gather | solution.py:122
  387.9 6.6 %multiply_reduce_fusion.1 = (f32[192,2,7]{0,2,1:T(8,128)S(1)}, bf16[192,2,7,128]{3,0,2,1:T(8,128)(2,1)}) fusion(bf16[192,2,7,128]{3,2,1,0:T(8,128)(2,1)S(1)} %copy-done.7, bf16[2,7,192,1536]{3,2,1,0:T(8,128)(2,1)} %copy-done.2, bf16[1536,2,128,1]{2,1,0,3:T(2,128)(2,1)S(1)} %bitcast.98), kind=kOutput, calls=%fused_computation.25 | convolution fusion | flops 1058682240 | bytes 10430976 | tf_op jit(solution)/shard_map/kgts,skd->tkgd/dot_general | solution.py:137
  394.6 9.5 %fusion.17 = f32[192,2,7,128]{3,0,2,1:T(8,128)} fusion(bf16[1536,2,128,1]{0,2,3,1:T(8,128)(2,1)} %bitcast.105, bf16[2,7,192,1536]{3,2,1,0:T(8,128)(2,1)} %copy-done.2, f32[2,7,192]{2,1,0:T(8,128)S(1)} %bitcast.107, bf16[1536,2,128,1]{2,1,0,3:T(2,128)(2,1)S(1)} %bitcast.99, bf16[192,2,7,128]{3,2,1,0:T(8,128)(2,1)S(1)} %copy-done.7), kind=kOutput, calls=%fused_computation.22 | convolution fusion | flops 2130788352 | bytes 11905536 | tf_op jit(solution)/shard_map/kgts,skd->tkgd/dot_general | solution.py:147
  404.0 2.3 subtract_convert_fusion
  416.3 136.6 %all-reduce.4.cloned.1.call-done = (f32[3584,64]{0,1:T(8,128)}, f32[64,1792]{1,0:T(8,128)}, f32[3584,64]{0,1:T(8,128)}, f32[64,256]{1,0:T(8,128)}) async-done(((f32[3584,64]{0,1:T(8,128)}, f32[64,1792]{1,0:T(8,128)}, f32[3584,64]{0,1:T(8,128)}, f32[64,256]{1,0:T(8,128)}), (f32[3584,64]{0,1:T(8,128)}, f32[64,1792]{1,0:T(8,128)}, f32[3584,64]{0,1:T(8,128)}, f32[64,256]{1,0:T(8,128)})) %all-reduce.4.cloned.1.call-update) | async-done | bytes 2359312 | tf_op jit(solution)/shard_map/psum | solution.py:167
  552.9 2.3 copy.105
  (108 shorter events, 53.6 us)
Async XLA Ops:
  7.2 248.6 %copy-start = (bf16[3584,448]{0,1:T(8,128)(2,1)S(1)}, bf16[3584,448]{0,1:T(8,128)(2,1)}, u32[]{:S(2)}) copy-start(bf16[3584,448]{0,1:T(8,128)(2,1)} %param.26) | copy-start | bytes 9633796
  7.2 74.7 %reduce-scatter.6.cloned.1.call-start = ((), (), s32[]{:S(2)}) async-start(), calls=%async_computation.4 | async-start | bytes 4276224 | tf_op jit(solution)/shard_map/reduce_scatter | solution.py:63
  7.2 10.2 %copy-start.9 = (bf16[4,16,1024]{2,1,0:T(8,128)(2,1)S(1)}, bf16[4,16,1024]{2,1,0:T(8,128)(2,1)}, u32[]{:S(2)}) copy-start(bf16[4,16,1024]{2,1,0:T(8,128)(2,1)} %param.18) | copy-start | bytes 393220
  29.9 92.9 %reduce-scatter.8.cloned.1.call-start = ((), (), s32[]{:S(2)}) async-start(), calls=%async_computation.5 | async-start | bytes 327680 | tf_op jit(solution)/shard_map/reduce_scatter | solution.py:72
  93.9 29.0 %copy-start.22 = (bf16[1,16,1024]{2,1,0:T(8,128)(2,1)S(1)}, bf16[1,16,1024]{2,1,0:T(8,128)(2,1)}, u32[]{:S(2)}) copy-start(bf16[1,16,1024]{2,1,0:T(8,128)(2,1)} %param.19) | copy-start | bytes 98308
  102.7 153.1 %all-gather.2.cloned.1.call-start = ((), (), s32[]{:S(2)}) async-start(), calls=%async_computation.6 | async-start | bytes 6881280 | tf_op jit(solution)/shard_map/all_gather | solution.py:90
  255.8 5.4 copy-start.4
  255.8 5.4 copy-start.14
  266.7 7.2 %copy-start.13 = (bf16[1,192,1792]{2,1,0:T(8,128)(2,1)S(1)}, bf16[1,192,1792]{2,1,0:T(8,128)(2,1)}, u32[]{:S(2)}) copy-start(bf16[1,192,1792]{2,1,0:T(8,128)(2,1)} %param.35) | copy-start | bytes 2064388
  266.7 50.3 %all-to-all-start = ((f32[4,192,576]{2,1,0:T(8,128)}), f32[4,192,576]{2,1,0:T(8,128)}, u32[]{:S(2)}, u32[]{:S(2)}) async-start(f32[4,192,576]{2,1,0:T(8,128)} %bitcast.4), calls=%async_computation.2 | async-start | bytes 3932160 | tf_op jit(solution)/shard_map/all_to_all | solution.py:99
  271.2 5.3 copy-start.3
  271.3 5.3 copy-start.16
  271.3 139.6 %reduce-scatter.10.cloned.1.call-start = ((), (), s32[]{:S(2)}) async-start(), calls=%async_computation.7 | async-start | bytes 1769472
  322.8 2.5 copy-start.10
  331.8 15.0 %copy-start.5 = (f32[192,2,7,64]{3,2,1,0:T(8,128)S(1)}, f32[192,2,7,64]{3,2,1,0:T(8,128)}, u32[]{:S(2)}) copy-start(f32[192,2,7,64]{3,2,1,0:T(8,128)} %get-tuple-element.15) | copy-start | bytes 2064388
  346.8 3.4 copy-start.19
  360.8 7.1 %copy-start.6 = (bf16[192,2,7,128]{3,2,1,0:T(8,128)(2,1)S(1)}, bf16[192,2,7,128]{3,2,1,0:T(8,128)(2,1)}, u32[]{:S(2)}) copy-start(bf16[192,2,7,128]{3,2,1,0:T(8,128)(2,1)} %reshape_squeeze.3) | copy-start | bytes 2064388
  367.9 3.2 copy-start.2
  372.8 180.1 %all-reduce.4.cloned.1.call-start = ((), (), s32[]{:S(2)}) async-start(), calls=%async_computation.8 | async-start | bytes 4718592 | tf_op jit(solution)/shard_map/psum | solution.py:167
  372.8 15.1 %copy-start.7 = (bf16[192,2,7,128]{3,2,1,0:T(8,128)(2,1)S(1)}, bf16[192,2,7,128]{3,2,1,0:T(8,128)(2,1)}, u32[]{:S(2)}) copy-start(bf16[192,2,7,128]{3,2,1,0:T(8,128)(2,1)} %reshape_squeeze.3) | copy-start | bytes 2064388
  394.6 9.5 %copy-start.18 = (f32[192,64]{1,0:T(8,128)S(1)}, f32[192,64]{1,0:T(8,128)}, u32[]{:S(2)}) copy-start(f32[192,64]{1,0:T(8,128)} %get-tuple-element.19) | copy-start | bytes 147460
  552.9 3.1 copy-start.12
  552.9 4.0 copy-start.21
  552.9 4.7 copy-start.1
  (6 other events, 11.3 us)
Sparse Core Ops, SparseCore 0:
  30.0 51.8 reduce-scatter.5
  102.8 19.9 reduce-scatter.7
  156.0 99.6 all-gather.1
  372.9 36.5 reduce-scatter.9
  415.9 136.9 all-reduce.3
where the time goes:
time: 573 us; the launch traced here: 564 us
  waiting for transfers between devices  347 us (61%)
  matrix products  81.1 us (14%)
  blocking collectives  59 us (10%)
  local copies, waits for them, and re-layouts  35.9 us (6%)
  other arithmetic  21.5 us (4%)
  between operations  15.1 us (3%)
    psum x1, waiting for transfers between devices, on_device(): lax.psum((part_aq, part_bq, part_av, part_bv), ('gx', 'gy'))  137 us
    all_gather x1, waiting for transfers between devices, on_device(): slab_rows = lax.all_gather(normal, 'gy', axis=0, tiled=True)  99.9 us
    reduce_scatter x1, waiting for transfers between devices, on_device(): lax.psum_scatter(jnp.concatenate([gate_part, up_part], axis=1), 'gx', sca...  52 us
    all_to_all x1, waiting for transfers between devices, on_device(): lax.all_to_all(projected, 'gy', split_axis=0, concat_axis=1, tiled=True)  38.4 us
    psum x1, blocking collectives, on_device(): bridge = lax.psum(bridge_part, 'gx').astype(jnp.bfloat16)  25.4 us
    reduce_scatter x1, waiting for transfers between devices, on_device(): lax.psum_scatter(partial_out, 'gy', scatter_dimension=0, tiled=True)  20.1 us
    all_gather x1, blocking collectives, on_device(): lax.all_gather(key_local, 'gx', axis=0, tiled=True)  11.6 us
  transfers between devices with their start and end apart: 6, of which 5 were waited for; matrix products, arithmetic and copies ran while one was open for 6% of the time, Pallas kernels for 0%

commit v1 on v0

--- a/solution.py
+++ b/solution.py
@@ -165,7 +165,7 @@
     part_aq = jnp.einsum("td,tr->dr", normal, dlow_query, preferred_element_type=jnp.float32)
     part_av = jnp.einsum("td,tr->dr", normal, dlow_value, preferred_element_type=jnp.float32)
     grad_aq, grad_bq, grad_av, grad_bv = lax.psum(
-        (part_aq, part_bq, part_av, part_bv), ("gx", "gy")
+        lax.psum((part_aq, part_bq, part_av, part_bv), "gy"), "gx"
     )
     attn_out = attended.reshape(1, tokens, HEADS * HD)
     return (attn_out, grad_aq, grad_bq, grad_av, grad_bv)

time: 573 us -> 594 us (1.037)
  waiting for transfers between devices: 347 us -> 367 us
    psum x1 -> x2, waiting for transfers between devices: 137 us -> 157 us  [the longest x1 93.3 us: on_device(): lax.psum((part_aq, part_bq, part_av, part_bv), 'gy')]
  transfers between devices with their start and end apart: 6 -> 7, of which waited for: 5 -> 6; matrix products, arithmetic and copies ran while one was open for 6% -> 6% of each run, Pallas kernels for 0% -> 0%
where the time goes in v1:
time: 594 us; the launch traced here: 585 us
  waiting for transfers between devices  367 us (62%)
  matrix products  81.1 us (14%)
  blocking collectives  59.2 us (10%)
  local copies, waits for them, and re-layouts  35.7 us (6%)
  other arithmetic  21.5 us (4%)
  between operations  15.4 us (3%)
    all_gather x1, waiting for transfers between devices, on_device(): slab_rows = lax.all_gather(normal, 'gy', axis=0, tiled=True)  99.9 us
    psum x1, waiting for transfers between devices, on_device(): lax.psum((part_aq, part_bq, part_av, part_bv), 'gy')  93.3 us
    psum x1, waiting for transfers between devices, on_device(): lax.psum(lax.psum((part_aq, part_bq, part_av, part_bv), 'gy'), 'gx')  63.8 us
    reduce_scatter x1, waiting for transfers between devices, on_device(): lax.psum_scatter(jnp.concatenate([gate_part, up_part], axis=1), 'gx', sca...  52 us
    all_to_all x1, waiting for transfers between devices, on_device(): lax.all_to_all(projected, 'gy', split_axis=0, concat_axis=1, tiled=True)  38.4 us
    psum x1, blocking collectives, on_device(): bridge = lax.psum(bridge_part, 'gx').astype(jnp.bfloat16)  25.4 us
    reduce_scatter x1, waiting for transfers between devices, on_device(): lax.psum_scatter(partial_out, 'gy', scatter_dimension=0, tiled=True)  20.1 us
  transfers between devices with their start and end apart: 7, of which 6 were waited for; matrix products, arithmetic and copies ran while one was open for 6% of the time, Pallas kernels for 0%

profile of v1, /device:TPU:0, one launch (start us, length us, event | category | flops | bytes accessed | tf_op | source)
XLA Modules:
  0.0 585.3 jit_solution(6433655267056165756)
XLA Ops:
  7.2 10.2 %fusion.54 = f32[64,7392]{1,0:T(8,128)S(1)} fusion(bf16[64,1024]{1,0:T(8,128)(2,1)} %bitcast.100, bf16[1024,7392]{0,1:T(8,128)(2,1)} %param.20), kind=kOutput, calls=%fused_computation.78 | convolution fusion | flops 968884224 | bytes 17162240 | tf_op jit(solution)/shard_map/dot_general | solution.py:61
  17.4 10.0 %fusion.55 = f32[64,7392]{1,0:T(8,128)S(1)} fusion(bf16[64,1024]{1,0:T(8,128)(2,1)S(1)} %bitcast.101, bf16[1024,7392]{0,1:T(8,128)(2,1)} %param.21), kind=kOutput, calls=%fused_computation.79 | convolution fusion | flops 968884224 | bytes 17162240 | tf_op jit(solution)/shard_map/dot_general | solution.py:62
  27.4 2.5 pad_maximum_fusion
  30.0 52.0 %reduce-scatter.6.cloned.1.call-done = f32[8,14784]{1,0:T(8,128)} async-done(((f32[64,14784]{1,0:T(8,128)}), f32[8,14784]{1,0:T(8,128)}) %reduce-scatter.6.cloned.1.call-update) | async-done | bytes 473104 | tf_op jit(solution)/shard_map/reduce_scatter | solution.py:63
  83.1 10.8 %all_gather.12 = bf16[64,7392]{1,0:T(8,128)(2,1)S(1)} all-gather(bf16[8,7392]{1,0:T(8,128)(2,1)S(1)} %fusion.32), channel_id=1, replica_groups=mesh['gx'=8,'gy'=4] {'gx'}, dimensions={0}, use_global_device_ids=true | all-gather | bytes 1064448 | tf_op jit(solution)/shard_map/all_gather | solution.py:68
  93.9 8.8 %fusion.56 = f32[64,1024]{1,0:T(8,128)} fusion(bf16[64,7392]{1,0:T(8,128)(2,1)S(1)} %all_gather.12, bf16[7392,1024]{1,0:T(8,128)(2,1)} %param.22), kind=kOutput, calls=%fused_computation.80 | convolution fusion | flops 968884224 | bytes 16347136 | tf_op jit(solution)/shard_map/dot_general | solution.py:67
  102.8 20.1 %reduce-scatter.8.cloned.1.call-done = f32[16,1024]{1,0:T(8,128)} async-done(((f32[64,1024]{1,0:T(8,128)}), f32[16,1024]{1,0:T(8,128)}) %reduce-scatter.8.cloned.1.call-update) | async-done | bytes 65552 | tf_op jit(solution)/shard_map/reduce_scatter | solution.py:72
  122.8 4.2 fusion.41
  127.0 25.4 %all-reduce.9 = bf16[16,3584]{1,0:T(8,128)(2,1)S(1)} all-reduce(f32[16,3584]{1,0:T(8,128)S(1)} %fusion.41), channel_id=1, replica_groups=mesh['gx'=8,'gy'=4] {'gx'}, use_global_device_ids=true, to_apply=%region_2.3 | all-reduce | flops 57344 | bytes 344064 | tf_op jit(solution)/shard_map/psum | solution.py:75
  155.9 99.9 %all-gather.2.cloned.1.call-done = bf16[768,3584]{1,0:T(8,128)(2,1)} async-done(((bf16[192,3584]{1,0:T(8,128)(2,1)}), bf16[768,3584]{1,0:T(8,128)(2,1)}) %all-gather.2.cloned.1.call-update) | async-done | bytes 5505040 | tf_op jit(solution)/shard_map/all_gather | solution.py:90
  255.8 5.4 fusion.57
  266.7 4.6 all-to-all-start
  278.7 38.4 %all-to-all-done = f32[4,192,576]{2,1,0:T(8,128)} async-done(((f32[4,192,576]{2,1,0:T(8,128)}), f32[4,192,576]{2,1,0:T(8,128)}, u32[]{:S(2)}, u32[]{:S(2)}) %all-to-all-start) | async-done | bytes 1769504 | tf_op jit(solution)/shard_map/all_to_all | solution.py:99
  322.9 2.5 reshape.208
  333.0 11.6 %all_gather.15 = bf16[1536,256]{1,0:T(8,128)(2,1)} all-gather(bf16[192,256]{1,0:T(8,128)(2,1)S(1)} %copy.50), channel_id=1, replica_groups=mesh['gx'=8,'gy'=4] {'gx'}, dimensions={0}, use_global_device_ids=true | all-gather | bytes 884736 | tf_op jit(solution)/shard_map/all_gather | solution.py:121
  346.9 3.4 subtract_convert_fusion.1
  350.3 10.6 %fusion.53 = (f32[2,7,192]{2,1,0:T(8,128)S(1)}, f32[2,7,192,1536]{3,2,1,0:T(8,128)}) fusion(pred[192,1536]{1,0:T(8,128)(4,1)S(1)} %copy-done.19, bf16[1536,2,128,1]{0,2,3,1:T(8,128)(2,1)} %bitcast.104, bf16[192,2,7,64]{3,0,2,1:T(8,128)(2,1)} %get-tuple-element.14, bf16[192,2,7,64]{3,0,2,1:T(8,128)(2,1)} %get-tuple-element.13), kind=kOutput, calls=%fused_computation.77 | convolution fusion | flops 1074857472 | bytes 18295296 | tf_op jit(solution)/shard_map/sub | solution.py:135
  360.9 7.1 %divide_convert_fusion = bf16[2,7,192,1536]{3,2,1,0:T(8,128)(2,1)S(1)} fusion(f32[2,7,192,1536]{3,2,1,0:T(8,128)} %get-tuple-element.29, f32[2,7,192]{2,1,0:T(8,128)S(1)} %get-tuple-element.28), kind=kLoop, calls=%fused_computation.5 | loop fusion | flops 8257536 | bytes 24783360 | tf_op jit(solution)/shard_map/convert_element_type | solution.py:136
  374.5 11.5 %all_gather.14 = bf16[1536,256]{1,0:T(8,128)(2,1)} all-gather(bf16[192,256]{1,0:T(8,128)(2,1)S(1)} %fusion.22), channel_id=1, replica_groups=mesh['gx'=8,'gy'=4] {'gx'}, dimensions={0}, use_global_device_ids=true | all-gather | bytes 884736 | tf_op jit(solution)/shard_map/all_gather | solution.py:122
  388.0 6.6 %multiply_reduce_fusion.1 = (f32[192,2,7]{0,2,1:T(8,128)S(1)}, bf16[192,2,7,128]{3,0,2,1:T(8,128)(2,1)}) fusion(bf16[192,2,7,128]{3,2,1,0:T(8,128)(2,1)S(1)} %copy-done.7, bf16[2,7,192,1536]{3,2,1,0:T(8,128)(2,1)} %copy-done.2, bf16[1536,2,128,1]{2,1,0,3:T(2,128)(2,1)S(1)} %bitcast.98), kind=kOutput, calls=%fused_computation.25 | convolution fusion | flops 1058682240 | bytes 10430976 | tf_op jit(solution)/shard_map/kgts,skd->tkgd/dot_general | solution.py:137
  394.7 9.5 %fusion.17 = f32[192,2,7,128]{3,0,2,1:T(8,128)} fusion(bf16[1536,2,128,1]{0,2,3,1:T(8,128)(2,1)} %bitcast.105, bf16[2,7,192,1536]{3,2,1,0:T(8,128)(2,1)} %copy-done.2, f32[2,7,192]{2,1,0:T(8,128)S(1)} %bitcast.107, bf16[1536,2,128,1]{2,1,0,3:T(2,128)(2,1)S(1)} %bitcast.99, bf16[192,2,7,128]{3,2,1,0:T(8,128)(2,1)S(1)} %copy-done.7), kind=kOutput, calls=%fused_computation.22 | convolution fusion | flops 2130788352 | bytes 11905536 | tf_op jit(solution)/shard_map/kgts,skd->tkgd/dot_general | solution.py:147
  404.1 2.3 subtract_convert_fusion
  414.4 93.3 %all-reduce.8.cloned.1.call-done = (f32[3584,64]{0,1:T(8,128)}, f32[64,1792]{1,0:T(8,128)}, f32[3584,64]{0,1:T(8,128)}, f32[64,256]{1,0:T(8,128)}) async-done(((f32[3584,64]{0,1:T(8,128)}, f32[64,1792]{1,0:T(8,128)}, f32[3584,64]{0,1:T(8,128)}, f32[64,256]{1,0:T(8,128)}), (f32[3584,64]{0,1:T(8,128)}, f32[64,1792]{1,0:T(8,128)}, f32[3584,64]{0,1:T(8,128)}, f32[64,256]{1,0:T(8,128)})) %all-reduce.8.cloned.1.call-update) | async-done | bytes 2359312 | tf_op jit(solution)/shard_map/psum | solution.py:168
  509.7 63.8 %all-reduce.6.cloned.1.call-done = (f32[3584,64]{0,1:T(8,128)}, f32[64,1792]{1,0:T(8,128)}, f32[3584,64]{0,1:T(8,128)}, f32[64,256]{1,0:T(8,128)}) async-done(((f32[3584,64]{0,1:T(8,128)}, f32[64,1792]{1,0:T(8,128)}, f32[3584,64]{0,1:T(8,128)}, f32[64,256]{1,0:T(8,128)}), (f32[3584,64]{0,1:T(8,128)}, f32[64,1792]{1,0:T(8,128)}, f32[3584,64]{0,1:T(8,128)}, f32[64,256]{1,0:T(8,128)})) %all-reduce.6.cloned.1.call-update) | async-done | bytes 2359312 | tf_op jit(solution)/shard_map/psum | solution.py:167
  (111 shorter events, 55.8 us)
Async XLA Ops:
  7.2 248.6 %copy-start = (bf16[3584,448]{0,1:T(8,128)(2,1)S(1)}, bf16[3584,448]{0,1:T(8,128)(2,1)}, u32[]{:S(2)}) copy-start(bf16[3584,448]{0,1:T(8,128)(2,1)} %param.26) | copy-start | bytes 9633796
  7.2 74.8 %reduce-scatter.6.cloned.1.call-start = ((), (), s32[]{:S(2)}) async-start(), calls=%async_computation.4 | async-start | bytes 4276224 | tf_op jit(solution)/shard_map/reduce_scatter | solution.py:63
  7.2 10.2 %copy-start.9 = (bf16[4,16,1024]{2,1,0:T(8,128)(2,1)S(1)}, bf16[4,16,1024]{2,1,0:T(8,128)(2,1)}, u32[]{:S(2)}) copy-start(bf16[4,16,1024]{2,1,0:T(8,128)(2,1)} %param.18) | copy-start | bytes 393220
  29.9 92.9 %reduce-scatter.8.cloned.1.call-start = ((), (), s32[]{:S(2)}) async-start(), calls=%async_computation.5 | async-start | bytes 327680 | tf_op jit(solution)/shard_map/reduce_scatter | solution.py:72
  93.9 29.0 %copy-start.22 = (bf16[1,16,1024]{2,1,0:T(8,128)(2,1)S(1)}, bf16[1,16,1024]{2,1,0:T(8,128)(2,1)}, u32[]{:S(2)}) copy-start(bf16[1,16,1024]{2,1,0:T(8,128)(2,1)} %param.19) | copy-start | bytes 98308
  102.7 153.1 %all-gather.2.cloned.1.call-start = ((), (), s32[]{:S(2)}) async-start(), calls=%async_computation.6 | async-start | bytes 6881280 | tf_op jit(solution)/shard_map/all_gather | solution.py:90
  255.8 5.4 copy-start.4
  255.8 5.4 copy-start.14
  266.7 7.2 %copy-start.13 = (bf16[1,192,1792]{2,1,0:T(8,128)(2,1)S(1)}, bf16[1,192,1792]{2,1,0:T(8,128)(2,1)}, u32[]{:S(2)}) copy-start(bf16[1,192,1792]{2,1,0:T(8,128)(2,1)} %param.35) | copy-start | bytes 2064388
  266.7 50.3 %all-to-all-start = ((f32[4,192,576]{2,1,0:T(8,128)}), f32[4,192,576]{2,1,0:T(8,128)}, u32[]{:S(2)}, u32[]{:S(2)}) async-start(f32[4,192,576]{2,1,0:T(8,128)} %bitcast.4), calls=%async_computation.2 | async-start | bytes 3932160 | tf_op jit(solution)/shard_map/all_to_all | solution.py:99
  271.3 5.3 copy-start.3
  271.3 5.3 copy-start.16
  271.3 139.7 %reduce-scatter.10.cloned.1.call-start = ((), (), s32[]{:S(2)}) async-start(), calls=%async_computation.7 | async-start | bytes 1769472
  331.8 15.0 %copy-start.5 = (f32[192,2,7,64]{3,2,1,0:T(8,128)S(1)}, f32[192,2,7,64]{3,2,1,0:T(8,128)}, u32[]{:S(2)}) copy-start(f32[192,2,7,64]{3,2,1,0:T(8,128)} %get-tuple-element.19) | copy-start | bytes 2064388
  346.9 3.4 copy-start.19
  360.9 7.1 %copy-start.6 = (bf16[192,2,7,128]{3,2,1,0:T(8,128)(2,1)S(1)}, bf16[192,2,7,128]{3,2,1,0:T(8,128)(2,1)}, u32[]{:S(2)}) copy-start(bf16[192,2,7,128]{3,2,1,0:T(8,128)(2,1)} %reshape_squeeze.3) | copy-start | bytes 2064388
  367.9 3.2 copy-start.2
  372.9 134.8 %all-reduce.8.cloned.1.call-start = ((), (), s32[]{:S(2)}) async-start(), calls=%async_computation.9 | async-start | bytes 4718592 | tf_op jit(solution)/shard_map/psum | solution.py:168
  372.9 15.1 %copy-start.7 = (bf16[192,2,7,128]{3,2,1,0:T(8,128)(2,1)S(1)}, bf16[192,2,7,128]{3,2,1,0:T(8,128)(2,1)}, u32[]{:S(2)}) copy-start(bf16[192,2,7,128]{3,2,1,0:T(8,128)(2,1)} %reshape_squeeze.3) | copy-start | bytes 2064388
  394.7 9.5 %copy-start.18 = (f32[192,64]{1,0:T(8,128)S(1)}, f32[192,64]{1,0:T(8,128)}, u32[]{:S(2)}) copy-start(f32[192,64]{1,0:T(8,128)} %get-tuple-element.23) | copy-start | bytes 147460
  414.3 93.4 %copy-start.8 = (bf16[192,2,7,128]{3,0,2,1:T(8,128)(2,1)S(1)}, bf16[192,2,7,128]{3,0,2,1:T(8,128)(2,1)}, u32[]{:S(2)}) copy-start(bf16[192,2,7,128]{3,0,2,1:T(8,128)(2,1)} %get-tuple-element.31) | copy-start | bytes 2064388
  414.3 159.2 %all-reduce.6.cloned.1.call-start = ((), (), s32[]{:S(2)}) async-start(), calls=%async_computation.8 | async-start | bytes 4718592 | tf_op jit(solution)/shard_map/psum | solution.py:167
  573.6 4.0 copy-start.21
  573.6 4.7 copy-start.1
  (7 other events, 15.4 us)
Sparse Core Ops, SparseCore 0:
  30.0 51.8 reduce-scatter.5
  102.8 19.9 reduce-scatter.7
  156.1 99.6 all-gather.1
  373.0 36.4 reduce-scatter.9
  414.4 93.1 all-reduce.7
  511.1 62.3 all-reduce.5
